TPU v7x, 32 devices: a whole 2x2x4 slice. The times are simulated.
32 devices in a mesh: tile: 8 (over y, x, core), mode: 4 (over z).
Axes of the slice: x: 2, y: 2, z: 4, core: 2. Of those that a mesh axis runs over, the one named last changes fastest.
Arguments:
- object_field: float32 [2, 2, 2048, 384], P(None, None, 'tile'), may hold values from -4 to 4
- probe: float32 [8, 2, 256, 256], P('mode'), may hold values from -4 to 4
- measured: float32 [32, 256, 256], P('tile'), may hold values from 0 to 16
- prop_phase: float32 [256, 256], replicated, may hold values from -3.140625 to 3.140625
- counts: int32 [8], P('tile'), may hold values from 1 to 4, 16 in all
- row_offset: int32 [32], P('tile'), may hold values from 0 to 255
- col_offset: int32 [32], P('tile'), may hold values from 0 to 128
Outputs:
- object_grad: float32 [2, 2, 2048, 384], P(None, None, 'tile')
- probe_grad: float32 [8, 2, 256, 256], P('mode')
Inputs may be any that keep to these rules, and one draw needn't show every extreme that they name: Slot i is live for i % 4 < counts[i // 4]; some tile has all 4 slots live.
All inputs are finite; a program needn't handle non-finite values. No bound on the sum of `counts` on one device may be relied on, other than what follows from the above.
Results may differ from a plain program's by a relative error of at most 0.0003.
Values sent between devices are 32-bit elements; how exact they have to be, the bound alone decides.
A program may use at most 128 MiB of HBM per device.

v0:
```python
import math
import jax
import jax.numpy as jnp
from jax import lax
from jax.sharding import PartitionSpec as P

MODES = 8
HIGH = lax.Precision.HIGHEST


def shifted(block, axis, distance):
    devices = range(lax.axis_size(axis))
    route = [(i - distance, i) for i in devices if i - distance in devices]
    return lax.ppermute(block, axis, route)


def dft_tables(length):
    indices = jnp.arange(length, dtype=jnp.int32)
    product = indices[:, None] * indices[None, :] % length
    angle = product.astype(jnp.float32) * (2.0 * math.pi / length)
    factor = 1.0 / math.sqrt(length)
    return (jnp.cos(angle) * factor, jnp.sin(angle) * factor)


def on_left(matrix, field):
    return jnp.einsum("jk,mkl->mjl", matrix, field, precision=HIGH)


def on_right(field, matrix):
    return jnp.einsum("mjk,kl->mjl", field, matrix, precision=HIGH)


def transform(pair, tables, sign):
    cosine, sine = tables
    real_in, imag_in = pair
    mid_real = on_left(cosine, real_in) - sign * on_left(sine, imag_in)
    mid_imag = on_left(cosine, imag_in) + sign * on_left(sine, real_in)
    out_real = on_right(mid_real, cosine) - sign * on_right(mid_imag, sine)
    out_imag = on_right(mid_imag, cosine) + sign * on_right(mid_real, sine)
    return (out_real, out_imag)


def times(first, second):
    return (
        first[0] * second[0] - first[1] * second[1],
        first[0] * second[1] + first[1] * second[0],
    )


def times_conj(first, second):
    return (
        first[0] * second[0] + first[1] * second[1],
        first[0] * second[1] - first[1] * second[0],
    )


def forward_pass(window, probe_pair, kernel, tables):
    wave = times(probe_pair, (window[0, 0], window[0, 1]))
    spectrum = transform(wave, tables, -1.0)
    moved = transform(times(kernel, spectrum), tables, 1.0)
    before = [moved]
    wave = times(moved, (window[1, 0], window[1, 1]))
    far_field = transform(wave, tables, -1.0)
    return (before, far_field)


def backward_pass(window, before, far_field, weight, probe_pair, kernel, tables):
    layers = window.shape[0]
    back = transform((weight * far_field[0], weight * far_field[1]), tables, 1.0)
    pieces = [None] * layers
    term = times_conj(before[0], back)
    pieces[1] = jnp.stack([jnp.sum(term[0], axis=0), jnp.sum(term[1], axis=0)])
    inner = transform(times_conj((window[1, 0], window[1, 1]), back), tables, -1.0)
    back = transform(times_conj(kernel, inner), tables, 1.0)
    first = times_conj(probe_pair, back)
    pieces[0] = jnp.stack([jnp.sum(first[0], axis=0), jnp.sum(first[1], axis=0)])
    probe_term = times_conj((window[0, 0], window[0, 1]), back)
    return (jnp.stack(pieces), jnp.stack([probe_term[0], probe_term[1]], axis=1))


def per_device(object_field, probe, measured, prop_phase, counts, row_offset, col_offset):
    layers, _, tile_rows, columns = object_field.shape
    width = probe.shape[-1]
    next_rows = shifted(object_field, "tile", -1)
    extended = jnp.concatenate([object_field, next_rows], axis=2)
    tables = dft_tables(width)
    kernel = (jnp.cos(prop_phase), jnp.sin(prop_phase))
    probe_pair = (probe[:, 0], probe[:, 1])
    live_count = counts[0]
    zero_index = jnp.zeros((), jnp.int32)
    slot_total = row_offset.shape[0]

    def cut_window(row_start, col_start):
        start = (zero_index, zero_index, row_start, col_start)
        return lax.dynamic_slice(extended, start, (layers, 2, width, width))

    def place_terms(grad_ext, pieces, row_start, col_start):
        start = (zero_index, zero_index, row_start, col_start)
        current = lax.dynamic_slice(grad_ext, start, (layers, 2, width, width))
        return lax.dynamic_update_slice(grad_ext, current + pieces, start)

    init = (jnp.zeros(extended.shape, jnp.float32), jnp.zeros(probe.shape, jnp.float32))
    windows = jax.vmap(cut_window)(row_offset, col_offset)
    before, far_field = jax.vmap(lambda item: forward_pass(item, probe_pair, kernel, tables))(
        windows
    )
    local_power = jnp.sum(far_field[0] * far_field[0] + far_field[1] * far_field[1], axis=1)
    power = lax.psum(local_power, "mode")
    alive = (jnp.arange(slot_total, dtype=jnp.int32) < live_count).astype(jnp.float32)
    weight = (power - measured) / MODES * alive[:, None, None]

    def one_back(item, item_before, item_far, item_weight):
        return backward_pass(item, item_before, item_far, item_weight, probe_pair, kernel, tables)

    all_pieces, probe_terms = jax.vmap(one_back)(windows, before, far_field, weight)
    grad_probe = jnp.sum(probe_terms, axis=0)

    def add_slot(slot, grad_ext):
        return place_terms(grad_ext, all_pieces[slot], row_offset[slot], col_offset[slot])

    grad_ext = lax.fori_loop(zero_index, jnp.full((), slot_total, jnp.int32), add_slot, init[0])
    summed = lax.psum(grad_ext, "mode")
    arrived = shifted(summed[:, :, tile_rows:, :], "tile", 1)
    object_grad = summed[:, :, :tile_rows, :].at[:, :, :width, :].add(arrived)
    probe_grad = lax.psum(grad_probe, "tile")
    return (object_grad, probe_grad)


def solution(mesh):
    placed = (
        P(None, None, "tile", None),
        P("mode", None, None, None),
        P("tile", None, None),
        P(),
        P("tile"),
        P("tile"),
        P("tile"),
    )
    return jax.shard_map(
        per_device,
        mesh=mesh,
        in_specs=placed,
        out_specs=(P(None, None, "tile", None), P("mode", None, None, None)),
        check_vma=False,
    )
```

profile of v0, /device:TPU:0, one launch (start us, length us, event | category | flops | bytes accessed | tf_op | source)
XLA Modules:
  0.0 612.1 jit_solution(3632968894506634922)
XLA Ops:
  16.6 12.5 %while.14 = (s32[]{:T(128)}, f32[2,2,512,384]{3,2,1,0:T(8,128)S(1)}, s32[4,4]{1,0:T(4,128)S(1)}, f32[4,2,2,256,256]{4,3,2,1,0:T(8,128)}, s32[]{:T(128)}) while((s32[]{:T(128)}, f32[2,2,512,384]{3,2,1,0:T(8,128)S(1)}, s32[4,4]{1,0:T(4,128)S(1)}, f32[4,2,2,256,256]{4,3,2,1,0:T(8,128)}, s32[]{:T(128)}) %tuple.57), condition=%wide.while_cond.1, body=%wide.while_body.1.sunk | while | flops 2 | bytes 2098801 | solution.py:95
  31.9 4.5 fusion.49
  40.8 4.6 multiply_add_fusion.9
  54.1 4.7 multiply_subtract_fusion.9
  58.8 4.5 multiply_add_fusion.8
  63.2 4.8 multiply_subtract_fusion.8
  68.1 4.6 fusion.116
  72.7 4.6 fusion.117
  77.3 4.8 convolution_add_fusion.1
  91.0 4.8 convolution_subtract_fusion.1
  95.9 4.5 fusion.70
  104.8 5.0 fusion.165
  109.9 4.6 fusion.162
  114.5 4.8 multiply_add_fusion.5
  128.3 4.8 multiply_subtract_fusion.5
  137.6 7.2 %add_reduce_fusion.2 = (f32[4,256,256]{2,1,0:T(8,128)}, f32[4,2,256,256]{3,2,1,0:T(8,128)}) fusion(f32[4,2,256,256]{3,2,1,0:T(8,128)S(1)} %multiply_subtract_fusion.4, f32[4,2,256,256]{3,2,1,0:T(8,128)S(1)} %fusion.24, f32[4,2,256,256]{3,2,1,0:T(8,128)S(1)} %multiply_subtract_fusion.5), kind=kOutput, calls=%fused_computation.70 | convolution fusion | flops 1614479360 | bytes 9437184 | tf_op jit(solution)/shard_map/vmap(mjk,kl->mjl)/dot_general | solution.py:30
  145.9 67.4 %all-reduce.4.cloned.1.call-done = f32[4,256,256]{2,1,0:T(8,128)} async-done(((f32[4,256,256]{2,1,0:T(8,128)}), f32[4,256,256]{2,1,0:T(8,128)}) %all-reduce.4.cloned.1.call-update) | async-done | bytes 1048592 | tf_op jit(solution)/shard_map/psum | solution.py:108
  215.5 4.5 fusion.54
  220.0 4.5 fusion.52
  224.5 4.7 fusion.63
  229.2 4.6 fusion.18
  233.8 4.6 fusion.16
  238.3 4.7 fusion.60
  243.1 4.5 fusion.80
  247.6 5.6 add_reduce_fusion
  253.2 4.6 fusion.155
  257.8 4.6 fusion.152
  262.5 4.8 multiply_add_fusion.2
  267.3 4.5 fusion.8
  271.8 4.5 fusion.10
  276.3 4.9 multiply_subtract_fusion.2
  281.2 4.6 multiply_add_fusion.1
  285.8 4.6 multiply_subtract_fusion.1
  290.4 5.0 fusion.118
  295.4 4.6 fusion.119
  300.0 4.8 convolution_add_fusion
  304.8 4.5 fusion.2
  309.3 4.5 fusion
  313.8 4.9 convolution_subtract_fusion
  318.7 4.5 fusion.90
  323.2 7.6 %add_bitcast_fusion = (f32[4,2,1,256,256]{4,3,1,0,2:T(8,128)S(1)}, f32[4,2,1,256,256]{4,3,1,0,2:T(8,128)}, f32[4,256,256]{2,1,0:T(8,128)S(1)}, f32[4,256,256]{2,1,0:T(8,128)S(1)}) fusion(f32[4,2,256,256]{3,2,1,0:T(8,128)S(1)} %fusion.90, f32[4,256,256]{2,1,0:T(8,128)S(1)} %get-tuple-element.89, f32[4,256,256]{2,1,0:T(8,128)S(1)} %copy-done.5, ...), kind=kOutput, calls=%fused_computation.57 | convolution fusion | flops 1618935808 | bytes 15728640 | tf_op jit(solution)/shard_map/vmap(mjk,kl->mjl)/dot_general | solution.py:30
  335.3 75.1 %while.13 = (s32[]{:T(128)}, f32[2,2,512,384]{3,2,1,0:T(8,128)}, s32[4]{0:T(128)S(1)}, s32[4]{0:T(128)S(1)}, f32[4,2,2,256,256]{4,3,2,1,0:T(8,128)}, /*index=5*/s32[]{:T(128)}, s32[]{:T(128)}, s32[]{:T(128)}, s32[]{:T(128)}) while((s32[]{:T(128)}, f32[2,2,512,384]{3,2,1,0:T(8,128)}, s32[4]{0:T(128)S(1)}, s32[4]{0:T(128)S(1)}, ...), condition=%wide.region_7.8_spmd, body=%wide.region_6.7_spmd.sunk | while | flops 262152 | bytes 5243081 | solution.py:121
  342.4 11.9 %dynamic_update_slice.4 = f32[2,2,512,384]{3,2,1,0:T(8,128)} dynamic-update-slice(f32[2,2,512,384]{3,2,1,0:T(8,128)} %get-tuple-element.186, f32[2,2,256,256]{3,2,1,0:T(8,128)S(1)} %bitcast_add_fusion.2, s32[]{:T(128)} %constant.72.clone.1..sunk, s32[]{:T(128)} %constant.72.clone.1..sunk, s32[]{:T(128)S(6)} %select_n.288, s32[]{:T(128)S(6)} %select_n.289) | dynamic-update-slice | bytes 2097156 | tf_op jit(solution)/shard_map/while/body/dynamic_update_slice | solution.py:100
  361.6 11.7 %dynamic_update_slice.4 = f32[2,2,512,384]{3,2,1,0:T(8,128)} dynamic-update-slice(f32[2,2,512,384]{3,2,1,0:T(8,128)} %get-tuple-element.186, f32[2,2,256,256]{3,2,1,0:T(8,128)S(1)} %bitcast_add_fusion.2, s32[]{:T(128)} %constant.72.clone.1..sunk, s32[]{:T(128)} %constant.72.clone.1..sunk, s32[]{:T(128)S(6)} %select_n.288, s32[]{:T(128)S(6)} %select_n.289) | dynamic-update-slice | bytes 2097156 | tf_op jit(solution)/shard_map/while/body/dynamic_update_slice | solution.py:100
  380.4 11.6 %dynamic_update_slice.4 = f32[2,2,512,384]{3,2,1,0:T(8,128)} dynamic-update-slice(f32[2,2,512,384]{3,2,1,0:T(8,128)} %get-tuple-element.186, f32[2,2,256,256]{3,2,1,0:T(8,128)S(1)} %bitcast_add_fusion.2, s32[]{:T(128)} %constant.72.clone.1..sunk, s32[]{:T(128)} %constant.72.clone.1..sunk, s32[]{:T(128)S(6)} %select_n.288, s32[]{:T(128)S(6)} %select_n.289) | dynamic-update-slice | bytes 2097156 | tf_op jit(solution)/shard_map/while/body/dynamic_update_slice | solution.py:100
  399.1 11.3 %dynamic_update_slice.4 = f32[2,2,512,384]{3,2,1,0:T(8,128)} dynamic-update-slice(f32[2,2,512,384]{3,2,1,0:T(8,128)} %get-tuple-element.186, f32[2,2,256,256]{3,2,1,0:T(8,128)S(1)} %bitcast_add_fusion.2, s32[]{:T(128)} %constant.72.clone.1..sunk, s32[]{:T(128)} %constant.72.clone.1..sunk, s32[]{:T(128)S(6)} %select_n.288, s32[]{:T(128)S(6)} %select_n.289) | dynamic-update-slice | bytes 2097156 | tf_op jit(solution)/shard_map/while/body/dynamic_update_slice | solution.py:100
  410.5 120.5 %all-reduce.6.cloned.1.call-done = f32[2,2,512,384]{3,2,1,0:T(8,128)} async-done(((f32[2,2,512,384]{3,2,1,0:T(8,128)}), f32[2,2,512,384]{3,2,1,0:T(8,128)}) %all-reduce.6.cloned.1.call-update) | async-done | bytes 3145744 | tf_op jit(solution)/shard_map/psum | solution.py:122
  537.8 62.4 %all-reduce.8.cloned.1.call-done = f32[2,2,256,256]{3,2,0,1:T(8,128)} async-done(((f32[2,2,256,256]{3,2,0,1:T(8,128)}), f32[2,2,256,256]{3,2,0,1:T(8,128)}) %all-reduce.8.cloned.1.call-update) | async-done | bytes 1048592 | tf_op jit(solution)/shard_map/psum | solution.py:125
  (104 shorter events, 96.6 us)
Async XLA Ops:
  7.2 206.1 %all-reduce.4.cloned.1.call-start = ((), (), s32[]{:S(2)}) async-start(), calls=%async_computation | async-start | bytes 2097152 | tf_op jit(solution)/shard_map/psum | solution.py:108
  7.2 7.8 %collective-permute-start = (f32[2,2,256,384]{3,2,1,0:T(8,128)}, f32[2,2,256,384]{3,2,1,0:T(8,128)}, u32[]{:S(2)}, u32[]{:S(2)}) collective-permute-start(f32[2,2,256,384]{3,2,1,0:T(8,128)} %param.13), channel_id=1, source_target_pairs={{4,0},{8,4},{12,8},{16,12},{20,16},{24,20},{28,24},{5,1},{9,5},{13... | collective-permute-start | bytes 4718600 | tf_op jit(solution)/shard_map/ppermute | solution.py:14
  10.0 5.0 copy-start.17
  29.2 2.7 copy-start.10
  29.2 2.7 copy-start.12
  31.9 22.2 %copy-start.4 = (f32[4,256,256]{2,1,0:T(8,128)}, f32[4,256,256]{2,1,0:T(8,128)S(1)}, u32[]{:S(2)}) copy-start(f32[4,256,256]{2,1,0:T(8,128)S(1)} %get-tuple-element.90) | copy-start | bytes 3145732
  63.2 4.9 copy-start.8
  100.3 27.9 %copy-start = (f32[4,2,256,256]{3,2,1,0:T(8,128)}, f32[4,2,256,256]{3,2,1,0:T(8,128)S(1)}, u32[]{:S(2)}) copy-start(f32[4,2,256,256]{3,2,1,0:T(8,128)S(1)} %fusion.70) | copy-start | bytes 6291460
  104.8 23.4 %copy-start.2 = (f32[4,2,256,256]{3,2,1,0:T(8,128)}, f32[4,2,256,256]{3,2,1,0:T(8,128)S(1)}, u32[]{:S(2)}) copy-start(f32[4,2,256,256]{3,2,1,0:T(8,128)S(1)} %fusion.73) | copy-start | bytes 6291460
  137.6 7.2 %copy-start.6 = (f32[4,2,256,256]{3,2,1,0:T(8,128)}, f32[4,2,256,256]{3,2,1,0:T(8,128)S(1)}, u32[]{:S(2)}) copy-start(f32[4,2,256,256]{3,2,1,0:T(8,128)S(1)} %multiply_subtract_fusion.4) | copy-start | bytes 6291460
  144.8 386.1 %all-reduce.6.cloned.1.call-start = ((), (), s32[]{:S(2)}) async-start(), calls=%async_computation.1 | async-start | bytes 6291456 | tf_op jit(solution)/shard_map/psum | solution.py:122
  213.3 2.2 copy-start.14
  220.0 4.5 copy-start.7
  243.1 4.5 copy-start.1
  243.1 4.5 copy-start.3
  285.8 4.6 copy-start.9
  318.7 4.5 copy-start.5
  318.7 4.5 copy-start.11
  318.7 4.5 copy-start.13
  333.4 1.9 copy-start.18
  333.4 1.9 copy-start.19
  410.4 189.7 %all-reduce.8.cloned.1.call-start = ((), (), s32[]{:S(2)}) async-start(), calls=%async_computation.2 | async-start | bytes 2097152 | tf_op jit(solution)/shard_map/psum | solution.py:125
  530.9 5.5 copy-start.15
  533.7 68.7 %collective-permute-start.1 = (f32[2,2,256,384]{3,2,1,0:T(8,128)}, f32[2,2,256,384]{3,2,1,0:T(8,128)}, u32[]{:S(2)}, u32[]{:S(2)}) collective-permute-start(f32[2,2,256,384]{3,2,1,0:T(8,128)} %slice.80), channel_id=1, source_target_pairs={{0,4},{4,8},{8,12},{12,16},{16,20},{20,24},{24,28},{1,5},{5,9},{9,... | collective-permute-start | bytes 4718600 | tf_op jit(solution)/shard_map/ppermute | solution.py:14
  537.7 64.7 %copy-start.16 = (f32[2,2,512,384]{3,2,1,0:T(8,128)S(1)}, f32[2,2,512,384]{3,2,1,0:T(8,128)}, u32[]{:S(2)}) copy-start(f32[2,2,512,384]{3,2,1,0:T(8,128)} %all-reduce.6.cloned.1.call-done) | copy-start | bytes 9437188
Sparse Core Ops, SparseCore 0:
  144.9 68.2 all-reduce.3
  410.6 120.3 all-reduce.5
  537.9 62.2 all-reduce.7
where the time goes:
time: 624 us; the launch traced here: 612 us
  waiting for transfers between devices  250 us (40%)
  matrix products  228 us (37%)
  local copies, waits for them, and re-layouts  78.8 us (13%)
  other arithmetic  19.9 us (3%)
  loops' own time  15.6 us (2%)
  between operations  15.4 us (2%)
    psum x1, waiting for transfers between devices, per_device(): summed = lax.psum(grad_ext, 'mode')  120 us
    dot_general x24, matrix products, on_right(): return jnp.einsum('mjk,kl->mjl', field, matrix, precision=HIGH)  115 us
    dot_general x24, matrix products, on_left(): return jnp.einsum('jk,mkl->mjl', matrix, field, precision=HIGH)  113 us
    psum x1, waiting for transfers between devices, per_device(): power = lax.psum(local_power, 'mode')  67.4 us
    psum x1, waiting for transfers between devices, per_device(): probe_grad = lax.psum(grad_probe, 'tile')  62.4 us
    dynamic_update_slice x4, local copies, waits for them, and re-layouts, place_terms(): return lax.dynamic_update_slice(grad_ext, current + pieces, start)  46.5 us
    another operation x1, loops' own time, per_device(): lax.fori_loop(zero_index, jnp.full((), slot_total, jnp.int32), add_slot,...  15.6 us
    gather x12, local copies, waits for them, and re-layouts  12.5 us
  transfers between devices with their start and end apart: 5, of which 3 were waited for; matrix products, arithmetic and copies ran while one was open for 2% of the time, Pallas kernels for 0%

commit v1 on v0

--- a/solution.py
+++ b/solution.py
@@ -119,7 +119,9 @@
         return place_terms(grad_ext, all_pieces[slot], row_offset[slot], col_offset[slot])
 
     grad_ext = lax.fori_loop(zero_index, jnp.full((), slot_total, jnp.int32), add_slot, init[0])
-    summed = lax.psum(grad_ext, "mode")
+    summed = grad_ext
+    for hop in (1, 2):
+        summed = summed + lax.ppermute(summed, "mode", [(dev, dev ^ hop) for dev in range(4)])
     arrived = shifted(summed[:, :, tile_rows:, :], "tile", 1)
     object_grad = summed[:, :, :tile_rows, :].at[:, :, :width, :].add(arrived)
     probe_grad = lax.psum(grad_probe, "tile")

time: 624 us -> 712 us (1.14)
  waiting for transfers between devices: 250 us -> 333 us
    ppermute x0 -> x2, waiting for transfers between devices: none -> 205 us  [per_device(): lax.ppermute(summed, 'mode', [(dev, dev ^ hop) for dev in range(4)])]
    psum x1 -> x0, waiting for transfers between devices: 120 us -> none  [per_device(): summed = lax.psum(grad_ext, 'mode')]
  transfers between devices with their start and end apart: 5 -> 6, of which waited for: 3 -> 4; matrix products, arithmetic and copies ran while one was open for 2% -> 1% of each run, Pallas kernels for 0% -> 0%
where the time goes in v1:
time: 712 us; the launch traced here: 700 us
  waiting for transfers between devices  333 us (47%)
  matrix products  228 us (32%)
  local copies, waits for them, and re-layouts  78.1 us (11%)
  other arithmetic  22.4 us (3%)
  between operations  15.8 us (2%)
  loops' own time  15.6 us (2%)
  starting transfers between devices  7.53 us (1%)
    ppermute x2, waiting for transfers between devices, per_device(): lax.ppermute(summed, 'mode', [(dev, dev ^ hop) for dev in range(4)])  205 us
    dot_general x24, matrix products, on_right(): return jnp.einsum('mjk,kl->mjl', field, matrix, precision=HIGH)  115 us
    dot_general x24, matrix products, on_left(): return jnp.einsum('jk,mkl->mjl', matrix, field, precision=HIGH)  113 us
    psum x1, waiting for transfers between devices, per_device(): power = lax.psum(local_power, 'mode')  67.3 us
    psum x1, waiting for transfers between devices, per_device(): probe_grad = lax.psum(grad_probe, 'tile')  60.2 us
    dynamic_update_slice x4, local copies, waits for them, and re-layouts, place_terms(): return lax.dynamic_update_slice(grad_ext, current + pieces, start)  46.4 us
    another operation x1, loops' own time, per_device(): lax.fori_loop(zero_index, jnp.full((), slot_total, jnp.int32), add_slot,...  15.6 us
  transfers between devices with their start and end apart: 6, of which 4 were waited for; matrix products, arithmetic and copies ran while one was open for 1% of the time, Pallas kernels for 0%

profile of v1, /device:TPU:0, one launch (start us, length us, event | category | flops | bytes accessed | tf_op | source)
XLA Modules:
  0.0 700.3 jit_solution(15197214526047287581)
XLA Ops:
  16.6 13.4 %while.14 = (s32[]{:T(128)}, f32[2,2,512,384]{3,2,1,0:T(8,128)S(1)}, s32[4,4]{1,0:T(4,128)S(1)}, f32[4,2,2,256,256]{4,3,2,1,0:T(8,128)}, s32[]{:T(128)}) while((s32[]{:T(128)}, f32[2,2,512,384]{3,2,1,0:T(8,128)S(1)}, s32[4,4]{1,0:T(4,128)S(1)}, f32[4,2,2,256,256]{4,3,2,1,0:T(8,128)}, s32[]{:T(128)}) %tuple.57), condition=%wide.while_cond.1, body=%wide.while_body.1.sunk | while | flops 2 | bytes 2098801 | solution.py:95
  32.8 4.5 fusion.49
  41.8 4.6 multiply_add_fusion.9
  55.0 4.7 multiply_subtract_fusion.9
  64.2 4.8 multiply_subtract_fusion.8
  69.0 4.6 fusion.116
  73.6 4.6 fusion.117
  78.2 4.8 convolution_add_fusion.1
  92.0 4.8 convolution_subtract_fusion.1
  96.8 4.5 fusion.70
  105.8 5.0 fusion.165
  110.8 4.6 fusion.162
  115.4 4.8 multiply_add_fusion.5
  129.2 4.8 multiply_subtract_fusion.5
  138.5 7.2 %add_reduce_fusion.2 = (f32[4,256,256]{2,1,0:T(8,128)}, f32[4,2,256,256]{3,2,1,0:T(8,128)}) fusion(f32[4,2,256,256]{3,2,1,0:T(8,128)S(1)} %multiply_subtract_fusion.4, f32[4,2,256,256]{3,2,1,0:T(8,128)S(1)} %fusion.24, f32[4,2,256,256]{3,2,1,0:T(8,128)S(1)} %multiply_subtract_fusion.5), kind=kOutput, calls=%fused_computation.70 | convolution fusion | flops 1614479360 | bytes 9437184 | tf_op jit(solution)/shard_map/vmap(mjk,kl->mjl)/dot_general | solution.py:30
  146.9 67.3 %all-reduce.3.cloned.1.call-done = f32[4,256,256]{2,1,0:T(8,128)} async-done(((f32[4,256,256]{2,1,0:T(8,128)}), f32[4,256,256]{2,1,0:T(8,128)}) %all-reduce.3.cloned.1.call-update) | async-done | bytes 1048592 | tf_op jit(solution)/shard_map/psum | solution.py:108
  216.4 4.5 fusion.54
  220.9 4.5 fusion.52
  225.4 4.7 fusion.63
  230.1 4.6 fusion.18
  234.7 4.6 fusion.16
  239.2 4.7 fusion.60
  244.0 4.5 fusion.80
  248.5 5.6 add_reduce_fusion
  254.1 4.6 fusion.155
  258.7 4.6 fusion.152
  263.4 4.8 multiply_add_fusion.2
  268.2 4.5 fusion.8
  272.7 4.5 fusion.10
  277.2 4.9 multiply_subtract_fusion.2
  282.1 4.6 multiply_add_fusion.1
  286.7 4.6 multiply_subtract_fusion.1
  291.3 5.0 fusion.118
  296.3 4.6 fusion.119
  300.9 4.8 convolution_add_fusion
  305.7 4.5 fusion.2
  310.2 4.5 fusion
  314.7 4.9 convolution_subtract_fusion
  319.6 4.5 fusion.90
  324.1 8.2 %add_bitcast_fusion = (f32[4,2,1,256,256]{4,3,1,0,2:T(8,128)}, f32[4,2,1,256,256]{4,3,1,0,2:T(8,128)}, f32[4,256,256]{2,1,0:T(8,128)S(1)}, f32[4,256,256]{2,1,0:T(8,128)S(1)}) fusion(f32[4,2,256,256]{3,2,1,0:T(8,128)S(1)} %fusion.90, f32[4,256,256]{2,1,0:T(8,128)S(1)} %get-tuple-element.89, f32[4,256,256]{2,1,0:T(8,128)S(1)} %copy-done.5, ...), kind=kOutput, calls=%fused_computation.57 | convolution fusion | flops 1618935808 | bytes 15728640 | tf_op jit(solution)/shard_map/vmap(mjk,kl->mjl)/dot_general | solution.py:30
  336.8 75.1 %while.13 = (s32[]{:T(128)}, f32[2,2,512,384]{3,2,1,0:T(8,128)}, s32[4]{0:T(128)S(1)}, s32[4]{0:T(128)S(1)}, f32[4,2,2,256,256]{4,3,2,1,0:T(8,128)}, /*index=5*/s32[]{:T(128)}, s32[]{:T(128)}, s32[]{:T(128)}, s32[]{:T(128)}) while((s32[]{:T(128)}, f32[2,2,512,384]{3,2,1,0:T(8,128)}, s32[4]{0:T(128)S(1)}, s32[4]{0:T(128)S(1)}, ...), condition=%wide.region_7.8_spmd, body=%wide.region_6.7_spmd.sunk | while | flops 262152 | bytes 5243081 | solution.py:121
  344.0 11.9 %dynamic_update_slice.4 = f32[2,2,512,384]{3,2,1,0:T(8,128)} dynamic-update-slice(f32[2,2,512,384]{3,2,1,0:T(8,128)} %get-tuple-element.186, f32[2,2,256,256]{3,2,1,0:T(8,128)S(1)} %bitcast_add_fusion.2, s32[]{:T(128)} %constant.72.clone.1..sunk, s32[]{:T(128)} %constant.72.clone.1..sunk, s32[]{:T(128)S(6)} %select_n.288, s32[]{:T(128)S(6)} %select_n.289) | dynamic-update-slice | bytes 2097156 | tf_op jit(solution)/shard_map/while/body/dynamic_update_slice | solution.py:100
  363.1 11.7 %dynamic_update_slice.4 = f32[2,2,512,384]{3,2,1,0:T(8,128)} dynamic-update-slice(f32[2,2,512,384]{3,2,1,0:T(8,128)} %get-tuple-element.186, f32[2,2,256,256]{3,2,1,0:T(8,128)S(1)} %bitcast_add_fusion.2, s32[]{:T(128)} %constant.72.clone.1..sunk, s32[]{:T(128)} %constant.72.clone.1..sunk, s32[]{:T(128)S(6)} %select_n.288, s32[]{:T(128)S(6)} %select_n.289) | dynamic-update-slice | bytes 2097156 | tf_op jit(solution)/shard_map/while/body/dynamic_update_slice | solution.py:100
  382.0 11.6 %dynamic_update_slice.4 = f32[2,2,512,384]{3,2,1,0:T(8,128)} dynamic-update-slice(f32[2,2,512,384]{3,2,1,0:T(8,128)} %get-tuple-element.186, f32[2,2,256,256]{3,2,1,0:T(8,128)S(1)} %bitcast_add_fusion.2, s32[]{:T(128)} %constant.72.clone.1..sunk, s32[]{:T(128)} %constant.72.clone.1..sunk, s32[]{:T(128)S(6)} %select_n.288, s32[]{:T(128)S(6)} %select_n.289) | dynamic-update-slice | bytes 2097156 | tf_op jit(solution)/shard_map/while/body/dynamic_update_slice | solution.py:100
  400.7 11.2 %dynamic_update_slice.4 = f32[2,2,512,384]{3,2,1,0:T(8,128)} dynamic-update-slice(f32[2,2,512,384]{3,2,1,0:T(8,128)} %get-tuple-element.186, f32[2,2,256,256]{3,2,1,0:T(8,128)S(1)} %bitcast_add_fusion.2, s32[]{:T(128)} %constant.72.clone.1..sunk, s32[]{:T(128)} %constant.72.clone.1..sunk, s32[]{:T(128)S(6)} %select_n.288, s32[]{:T(128)S(6)} %select_n.289) | dynamic-update-slice | bytes 2097156 | tf_op jit(solution)/shard_map/while/body/dynamic_update_slice | solution.py:100
  413.3 69.3 %collective-permute-done.1 = f32[2,2,512,384]{3,2,1,0:T(8,128)S(1)} collective-permute-done((f32[2,2,512,384]{3,2,1,0:T(8,128)}, f32[2,2,512,384]{3,2,1,0:T(8,128)S(1)}, u32[]{:S(2)}, u32[]{:S(2)}) %collective-permute-start.1) | collective-permute-done | bytes 3145760 | tf_op jit(solution)/shard_map/ppermute | solution.py:124
  486.0 135.8 %collective-permute-done.2 = f32[2,2,512,384]{3,2,1,0:T(8,128)S(1)} collective-permute-done((f32[2,2,512,384]{3,2,1,0:T(8,128)S(1)}, f32[2,2,512,384]{3,2,1,0:T(8,128)S(1)}, u32[]{:S(2)}, u32[]{:S(2)}) %collective-permute-start.2) | collective-permute-done | bytes 3145760 | tf_op jit(solution)/shard_map/ppermute | solution.py:124
  627.9 60.2 %all-reduce.5.cloned.1.call-done = f32[2,2,256,256]{3,2,0,1:T(8,128)} async-done(((f32[2,2,256,256]{3,2,0,1:T(8,128)}), f32[2,2,256,256]{3,2,0,1:T(8,128)}) %all-reduce.5.cloned.1.call-update) | async-done | bytes 1048592 | tf_op jit(solution)/shard_map/psum | solution.py:127
  (107 shorter events, 105.9 us)
Async XLA Ops:
  7.2 207.0 %all-reduce.3.cloned.1.call-start = ((), (), s32[]{:S(2)}) async-start(), calls=%async_computation | async-start | bytes 2097152 | tf_op jit(solution)/shard_map/psum | solution.py:108
  7.2 7.8 %collective-permute-start = (f32[2,2,256,384]{3,2,1,0:T(8,128)}, f32[2,2,256,384]{3,2,1,0:T(8,128)}, u32[]{:S(2)}, u32[]{:S(2)}) collective-permute-start(f32[2,2,256,384]{3,2,1,0:T(8,128)} %param.13), channel_id=1, source_target_pairs={{4,0},{8,4},{12,8},{16,12},{20,16},{24,20},{28,24},{5,1},{9,5},{13... | collective-permute-start | bytes 4718600 | tf_op jit(solution)/shard_map/ppermute | solution.py:14
  10.0 5.0 copy-start.17
  30.1 2.7 copy-start.10
  30.1 2.7 copy-start.12
  32.8 22.2 %copy-start.4 = (f32[4,256,256]{2,1,0:T(8,128)}, f32[4,256,256]{2,1,0:T(8,128)S(1)}, u32[]{:S(2)}) copy-start(f32[4,256,256]{2,1,0:T(8,128)S(1)} %get-tuple-element.90) | copy-start | bytes 3145732
  64.2 4.9 copy-start.8
  101.3 27.9 %copy-start = (f32[4,2,256,256]{3,2,1,0:T(8,128)}, f32[4,2,256,256]{3,2,1,0:T(8,128)S(1)}, u32[]{:S(2)}) copy-start(f32[4,2,256,256]{3,2,1,0:T(8,128)S(1)} %fusion.70) | copy-start | bytes 6291460
  105.7 23.4 %copy-start.2 = (f32[4,2,256,256]{3,2,1,0:T(8,128)}, f32[4,2,256,256]{3,2,1,0:T(8,128)S(1)}, u32[]{:S(2)}) copy-start(f32[4,2,256,256]{3,2,1,0:T(8,128)S(1)} %fusion.73) | copy-start | bytes 6291460
  138.5 7.2 %copy-start.6 = (f32[4,2,256,256]{3,2,1,0:T(8,128)}, f32[4,2,256,256]{3,2,1,0:T(8,128)S(1)}, u32[]{:S(2)}) copy-start(f32[4,2,256,256]{3,2,1,0:T(8,128)S(1)} %multiply_subtract_fusion.4) | copy-start | bytes 6291460
  145.8 542.3 %all-reduce.5.cloned.1.call-start = ((), (), s32[]{:S(2)}) async-start(), calls=%async_computation.1 | async-start | bytes 2097152 | tf_op jit(solution)/shard_map/psum | solution.py:127
  214.2 2.2 copy-start.14
  220.9 4.5 copy-start.7
  244.0 4.5 copy-start.1
  244.0 4.5 copy-start.3
  286.7 4.6 copy-start.9
  319.6 4.5 copy-start.5
  319.6 4.5 copy-start.11
  319.6 4.5 copy-start.13
  334.9 1.9 copy-start.18
  334.9 1.9 copy-start.19
  411.9 70.6 %collective-permute-start.1 = (f32[2,2,512,384]{3,2,1,0:T(8,128)}, f32[2,2,512,384]{3,2,1,0:T(8,128)S(1)}, u32[]{:S(2)}, u32[]{:S(2)}) collective-permute-start(f32[2,2,512,384]{3,2,1,0:T(8,128)} %get-tuple-element.49), channel_id=1, source_target_pairs={{0,1},{1,0},{2,3},{3,2},{4,5},{5,4},{6,7},{7,6},{8,9},{9,8},{10,11... | collective-permute-start | bytes 9437192 | tf_op jit(solution)/shard_map/ppermute | solution.py:124
  484.8 137.0 %collective-permute-start.2 = (f32[2,2,512,384]{3,2,1,0:T(8,128)S(1)}, f32[2,2,512,384]{3,2,1,0:T(8,128)S(1)}, u32[]{:S(2)}, u32[]{:S(2)}) collective-permute-start(f32[2,2,512,384]{3,2,1,0:T(8,128)S(1)} %add.252), channel_id=1, source_target_pairs={{0,2},{1,3},{2,0},{3,1},{4,6},{5,7},{6,4},{7,5},{8,10},{9,11},{10,... | collective-permute-start | bytes 9437192 | tf_op jit(solution)/shard_map/ppermute | solution.py:124
  621.8 4.8 copy-start.16
  622.1 4.5 copy-start.15
  623.4 67.0 %collective-permute-start.3 = (f32[2,2,256,384]{3,2,1,0:T(8,128)}, f32[2,2,256,384]{3,2,1,0:T(8,128)}, u32[]{:S(2)}, u32[]{:S(2)}) collective-permute-start(f32[2,2,256,384]{3,2,1,0:T(8,128)} %slice.80), channel_id=1, source_target_pairs={{0,4},{4,8},{8,12},{12,16},{16,20},{20,24},{24,28},{1,5},{5,9},{9,... | collective-permute-start | bytes 4718600 | tf_op jit(solution)/shard_map/ppermute | solution.py:14
Sparse Core Ops, SparseCore 0:
  145.9 68.2 all-reduce.2
  628.0 59.9 all-reduce.4
